TPU v7x, 32 devices: a whole 2x2x4 slice. The times are simulated.
32 devices in a mesh: dp: 8 (over z, core), tensor: 4 (over y, x).
Axes of the slice: x: 2, y: 2, z: 4, core: 2. Of those that a mesh axis runs over, the one named last changes fastest.
Arguments:
- block_input: bfloat16 [8192, 2048], P('dp'), may hold values from -6 to 6
- block_owner: int32 [64], P('dp'), may hold values from 0 to 63, as said below
- token_mask: int32 [8192], P('dp'), may hold values from 0 to 1, as said below
- attention_gain: float32 [2048], replicated, may hold values from 0.5 to 1.5
- query_weight: bfloat16 [2048, 2048], P(None, 'tensor')
- key_weight: bfloat16 [2048, 2048], P(None, 'tensor')
- value_weight: bfloat16 [2048, 2048], P(None, 'tensor'), may hold values from -0.125 to 0.125
- output_weight: bfloat16 [2048, 2048], P('tensor'), may hold values from -0.5 to 0.5
- feedforward_gain: float32 [2048], replicated, may hold values from 0.5 to 1.5
- gate_weight: bfloat16 [2048, 8192], P(None, 'tensor'), may hold values from -0.125 to 0.125
- up_weight: bfloat16 [2048, 8192], P(None, 'tensor'), may hold values from -0.125 to 0.125
- down_weight: bfloat16 [8192, 2048], P('tensor'), may hold values from -0.0625 to 0.0625
- cotangent: bfloat16 [8192, 2048], P('dp'), may hold values from -6 to 6
Outputs:
- block_output: bfloat16 [8192, 2048], P('dp')
- input_gradient: float32 [8192, 2048], P('dp')
- attention_gain_gradient: float32 [2048], P('dp')
- query_gradient: float32 [2048, 2048], P('dp', 'tensor')
- key_gradient: float32 [2048, 2048], P('dp', 'tensor')
- value_gradient: float32 [2048, 2048], P('dp', 'tensor')
- output_gradient: float32 [2048, 2048], P('tensor', 'dp')
- feedforward_gain_gradient: float32 [2048], P('dp')
- gate_gradient: float32 [2048, 8192], P('dp', 'tensor')
- up_gradient: float32 [2048, 8192], P('dp', 'tensor')
- down_gradient: float32 [8192, 2048], P('tensor', 'dp')
Inputs may be any that keep to these rules, and one draw needn't show every extreme that they name: `block_owner`: each sequence takes one to 4 consecutive blocks of a single index of dp; a block's entry is the index of its sequence's first block in the whole array. The first 4 blocks of every index of dp form one sequence. `token_mask`: in each sequence the real tokens come first and there is at least one unless the sequence is a single block of padding; the first sequence of every index of dp is all real (512 tokens). Blocks after the last real token of an index of dp are padding, each its own sequence.
All inputs are finite; a program needn't handle non-finite values.
Results may differ from a plain program's by a relative error of at most 0.014.
Values sent between devices are 32-bit elements; how exact they have to be, the bound alone decides.
No kernel may reach another device: no remote copies, remote signals or barrier semaphores. Data moves between devices by JAX's collectives and lax.ppermute only.
A program may use at most 384 MiB of HBM per device.

v0:
```python
import jax
import jax.numpy as jnp
from jax import lax
from jax.sharding import PartitionSpec as P

HD = 64
BLK = 128
GROUP = 512
WINDOW = 896
NORM_EPS = 1e-05
ROPE_BASE = 130000.0
MASKED = -1e30


def rms_forward(values, norm_gain):
    inverse = lax.rsqrt(jnp.mean(values * values, axis=-1, keepdims=True) + NORM_EPS)
    return (values * inverse * norm_gain, inverse)


def rms_backward(values, inverse, norm_gain, upstream):
    unit_rows = values * inverse
    gain_part = jnp.sum(upstream * unit_rows, axis=0)
    scaled = upstream * norm_gain
    back = inverse * (scaled - unit_rows * jnp.mean(scaled * unit_rows, axis=-1, keepdims=True))
    return (back, gain_part)


def rope_tables(positions, width):
    half_width = width // 2
    frequency = ROPE_BASE ** (-(jnp.arange(half_width, dtype=jnp.float32) * 2.0 / width))
    angles = positions.astype(jnp.float32)[:, None] * frequency[None, :]
    return (jnp.cos(angles)[:, None, :], jnp.sin(angles)[:, None, :])


def rotate(values, cosine, sine):
    half_width = values.shape[-1] // 2
    first_half = values[..., :half_width]
    second_half = values[..., half_width:]
    return jnp.concatenate(
        [first_half * cosine - second_half * sine, second_half * cosine + first_half * sine],
        axis=-1,
    )


def allowed_keys(query_owner, query_pos, key_owner, key_pos, key_valid):
    same = query_owner[:, None] == key_owner[None, :]
    causal = key_pos[None, :] <= query_pos[:, None]
    usable = (key_valid[None, :] > 0) | (key_pos[None, :] == 0)
    return same & causal & usable


def masked_scores(query_block, key_block, allowed, scale):
    scores = (
        jnp.einsum("qhd,khd->hqk", query_block, key_block, preferred_element_type=jnp.float32)
        * scale
    )
    return jnp.where(allowed[None], scores, MASKED)


def on_device(
    block_input,
    block_owner,
    token_mask,
    attention_gain,
    query_weight,
    key_weight,
    value_weight,
    output_weight,
    feedforward_gain,
    gate_weight,
    up_weight,
    down_weight,
    cotangent,
):
    row_count = block_input.shape[0]
    head_count = query_weight.shape[1] // HD
    scale = HD ** (-0.5)
    front = WINDOW - GROUP
    group_count = row_count // GROUP
    first_block = lax.axis_index("dp") * (row_count // BLK)
    owners = jnp.repeat(block_owner, BLK, total_repeat_length=row_count)
    row_index = jnp.arange(row_count, dtype=jnp.int32)
    positions = (row_index // BLK + first_block - owners) * BLK + row_index % BLK
    cosine, sine = rope_tables(positions, HD)
    key_owner = jnp.concatenate([jnp.full((front,), -1, jnp.int32), owners])
    key_pos = jnp.concatenate([jnp.zeros((front,), jnp.int32), positions])
    key_valid = jnp.concatenate([jnp.zeros((front,), jnp.int32), token_mask])
    group_masks = []
    for group in range(group_count):
        start = group * GROUP
        group_masks.append(
            allowed_keys(
                owners[start : start + GROUP],
                positions[start : start + GROUP],
                key_owner[start : start + WINDOW],
                key_pos[start : start + WINDOW],
                key_valid[start : start + WINDOW],
            )
        )
    inputs_f = block_input.astype(jnp.float32)
    normed_one, inverse_one = rms_forward(inputs_f, attention_gain)
    act_one = normed_one.astype(jnp.bfloat16)

    def project(weight):
        return jnp.dot(act_one, weight, preferred_element_type=jnp.float32).reshape(
            row_count, head_count, HD
        )

    queries = rotate(project(query_weight), cosine, sine).astype(jnp.bfloat16)
    keys_rot = rotate(project(key_weight), cosine, sine).astype(jnp.bfloat16)
    values_b = project(value_weight).astype(jnp.bfloat16)
    pad_block = jnp.zeros((front, head_count, HD), jnp.bfloat16)
    key_pad = jnp.concatenate([pad_block, keys_rot], axis=0)
    value_pad = jnp.concatenate([pad_block, values_b], axis=0)
    attn_list = []
    logsum_list = []
    for group in range(group_count):
        start = group * GROUP
        scores = masked_scores(
            queries[start : start + GROUP],
            key_pad[start : start + WINDOW],
            group_masks[group],
            scale,
        )
        peak = jnp.max(scores, axis=-1, keepdims=True)
        logsum = peak + jnp.log(jnp.sum(jnp.exp(scores - peak), axis=-1, keepdims=True))
        probs = jnp.exp(scores - logsum).astype(jnp.bfloat16)
        result = jnp.einsum(
            "hqk,khd->qhd",
            probs,
            value_pad[start : start + WINDOW],
            preferred_element_type=jnp.float32,
        )
        attn_list.append(result.astype(jnp.bfloat16))
        logsum_list.append(logsum)
    attn_heads = jnp.concatenate(attn_list, axis=0)
    attn_flat = attn_heads.reshape(row_count, head_count * HD)
    attn_part = jnp.dot(attn_flat, output_weight, preferred_element_type=jnp.float32)
    attn_total = lax.psum(attn_part, "tensor")
    hidden_sum = inputs_f + attn_total
    normed_two, inverse_two = rms_forward(hidden_sum, feedforward_gain)
    act_two = normed_two.astype(jnp.bfloat16)
    gate_pre = jnp.dot(act_two, gate_weight, preferred_element_type=jnp.float32)
    up_pre = jnp.dot(act_two, up_weight, preferred_element_type=jnp.float32)
    sigmoid_gate = jax.nn.sigmoid(gate_pre)
    inner = (gate_pre * sigmoid_gate * up_pre).astype(jnp.bfloat16)
    mlp_part = jnp.dot(inner, down_weight, preferred_element_type=jnp.float32)
    mlp_total = lax.psum(mlp_part, "tensor")
    block_output = (hidden_sum + mlp_total).astype(jnp.bfloat16)
    grad_rows = jnp.where(token_mask[:, None] > 0, cotangent, jnp.zeros_like(cotangent))
    down_grad = jnp.dot(inner.T, grad_rows, preferred_element_type=jnp.float32)
    inner_grad = jnp.dot(grad_rows, down_weight.T, preferred_element_type=jnp.float32)
    gate_back = (
        inner_grad * up_pre * sigmoid_gate * (1.0 + gate_pre * (1.0 - sigmoid_gate))
    ).astype(jnp.bfloat16)
    up_back = (inner_grad * gate_pre * sigmoid_gate).astype(jnp.bfloat16)
    gate_grad = jnp.dot(act_two.T, gate_back, preferred_element_type=jnp.float32)
    up_grad = jnp.dot(act_two.T, up_back, preferred_element_type=jnp.float32)
    act_two_part = jnp.dot(gate_back, gate_weight.T, preferred_element_type=jnp.float32) + jnp.dot(
        up_back, up_weight.T, preferred_element_type=jnp.float32
    )
    act_two_grad = lax.psum(act_two_part, "tensor")
    hidden_norm_back, second_gain_grad = rms_backward(
        hidden_sum, inverse_two, feedforward_gain, act_two_grad
    )
    hidden_grad = grad_rows.astype(jnp.float32) + hidden_norm_back
    mlp_summed = (
        lax.psum_scatter(gate_grad, "dp", scatter_dimension=0, tiled=True),
        lax.psum_scatter(up_grad, "dp", scatter_dimension=0, tiled=True),
        lax.psum_scatter(down_grad, "dp", scatter_dimension=1, tiled=True),
        lax.psum_scatter(second_gain_grad, "dp", scatter_dimension=0, tiled=True),
    )
    hidden_back = hidden_grad.astype(jnp.bfloat16)
    out_grad = jnp.dot(attn_flat.T, hidden_back, preferred_element_type=jnp.float32)
    attention_grad = (
        jnp.dot(hidden_back, output_weight.T, preferred_element_type=jnp.float32)
        .astype(jnp.bfloat16)
        .reshape(row_count, head_count, HD)
    )
    key_acc = jnp.zeros((front + row_count, head_count, HD), jnp.float32)
    value_acc = jnp.zeros((front + row_count, head_count, HD), jnp.float32)
    query_parts = []
    for group in range(group_count):
        start = group * GROUP
        query_block = queries[start : start + GROUP]
        key_block = key_pad[start : start + WINDOW]
        value_block = value_pad[start : start + WINDOW]
        grad_block = attention_grad[start : start + GROUP]
        scores = masked_scores(query_block, key_block, group_masks[group], scale)
        probs_f = jnp.exp(scores - logsum_list[group])
        probs_b = probs_f.astype(jnp.bfloat16)
        value_acc = value_acc.at[start : start + WINDOW].add(
            jnp.einsum("hqk,qhd->khd", probs_b, grad_block, preferred_element_type=jnp.float32)
        )
        prob_grad = jnp.einsum(
            "qhd,khd->hqk", grad_block, value_block, preferred_element_type=jnp.float32
        )
        delta = jnp.sum(
            grad_block.astype(jnp.float32) * attn_heads[start : start + GROUP].astype(jnp.float32),
            axis=-1,
        ).T[:, :, None]
        score_grad = (probs_f * (prob_grad - delta) * scale).astype(jnp.bfloat16)
        query_parts.append(
            jnp.einsum("hqk,khd->qhd", score_grad, key_block, preferred_element_type=jnp.float32)
        )
        key_acc = key_acc.at[start : start + WINDOW].add(
            jnp.einsum("hqk,qhd->khd", score_grad, query_block, preferred_element_type=jnp.float32)
        )
    query_back = (
        rotate(jnp.concatenate(query_parts, axis=0), cosine, -sine)
        .astype(jnp.bfloat16)
        .reshape(row_count, head_count * HD)
    )
    key_back = (
        rotate(key_acc[front:], cosine, -sine)
        .astype(jnp.bfloat16)
        .reshape(row_count, head_count * HD)
    )
    value_back = value_acc[front:].astype(jnp.bfloat16).reshape(row_count, head_count * HD)
    query_grad = jnp.dot(act_one.T, query_back, preferred_element_type=jnp.float32)
    key_grad = jnp.dot(act_one.T, key_back, preferred_element_type=jnp.float32)
    value_grad = jnp.dot(act_one.T, value_back, preferred_element_type=jnp.float32)
    act_one_part = (
        jnp.dot(query_back, query_weight.T, preferred_element_type=jnp.float32)
        + jnp.dot(key_back, key_weight.T, preferred_element_type=jnp.float32)
        + jnp.dot(value_back, value_weight.T, preferred_element_type=jnp.float32)
    )
    act_one_grad = lax.psum(act_one_part, "tensor")
    input_norm_back, first_gain_grad = rms_backward(
        inputs_f, inverse_one, attention_gain, act_one_grad
    )
    input_gradient = hidden_grad + input_norm_back
    first_summed = (
        lax.psum_scatter(first_gain_grad, "dp", scatter_dimension=0, tiled=True),
        lax.psum_scatter(query_grad, "dp", scatter_dimension=0, tiled=True),
        lax.psum_scatter(key_grad, "dp", scatter_dimension=0, tiled=True),
        lax.psum_scatter(value_grad, "dp", scatter_dimension=0, tiled=True),
        lax.psum_scatter(out_grad, "dp", scatter_dimension=1, tiled=True),
    )
    gate_sum, up_sum, down_sum, second_gain_sum = mlp_summed
    first_gain_sum, query_sum, key_sum, value_sum, out_sum = first_summed
    return (
        block_output,
        input_gradient,
        first_gain_sum,
        query_sum,
        key_sum,
        value_sum,
        out_sum,
        second_gain_sum,
        gate_sum,
        up_sum,
        down_sum,
    )


def solution(mesh):
    return jax.shard_map(
        on_device,
        mesh=mesh,
        in_specs=(
            P("dp", None),
            P("dp"),
            P("dp"),
            P(),
            P(None, "tensor"),
            P(None, "tensor"),
            P(None, "tensor"),
            P("tensor", None),
            P(),
            P(None, "tensor"),
            P(None, "tensor"),
            P("tensor", None),
            P("dp", None),
        ),
        out_specs=(
            P("dp", None),
            P("dp", None),
            P("dp"),
            P("dp", "tensor"),
            P("dp", "tensor"),
            P("dp", "tensor"),
            P("tensor", "dp"),
            P("dp"),
            P("dp", "tensor"),
            P("dp", "tensor"),
            P("tensor", "dp"),
        ),
        check_vma=False,
    )
```

profile of v0, /device:TPU:0, one launch (start us, length us, event | category | flops | bytes accessed | tf_op | source)
XLA Modules:
  0.0 1614.1 jit_solution(13321575594222905438)
XLA Ops:
  8.9 4.5 compare_select_fusion.1
  14.1 3.1 fusion.14
  17.2 5.5 fusion.72
  22.8 2.6 fusion.70
  28.0 2.8 fusion.6
  30.8 4.0 exponential_reduce_fusion.1
  34.8 2.6 convolution_convert_fusion
  38.0 6.8 fusion.7
  44.8 7.3 exponential_reduce_fusion
  52.3 4.1 fusion.24
  56.4 7.5 fusion.25
  65.7 5.8 fusion.81
  71.6 174.8 %all-reduce.15.cloned.1.call-done = f32[1024,2048]{1,0:T(8,128)} async-done(((f32[1024,2048]{1,0:T(8,128)}), f32[1024,2048]{1,0:T(8,128)}) %all-reduce.15.cloned.1.call-update) | async-done | bytes 8388624 | tf_op jit(solution)/shard_map/psum | solution.py:139
  246.5 5.7 multiply_reduce_fusion.2
  253.0 16.5 %fusion.82 = f32[1024,2048]{1,0:T(8,128)} fusion(bf16[1024,2048]{1,0:T(8,128)(2,1)S(1)} %multiply_convert_fusion.5, bf16[2048,2048]{1,0:T(8,128)(2,1)} %param.32), kind=kOutput, calls=%fused_computation.154 | convolution fusion | flops 8589934592 | bytes 20971520 | tf_op jit(solution)/shard_map/dot_general | solution.py:143
  269.5 13.3 fusion.83
  282.9 21.9 %multiply_convert_fusion.2 = (bf16[1024,2048]{1,0:T(8,128)(2,1)}, bf16[1024,2048]{1,0:T(8,128)(2,1)}, bf16[1024,2048]{1,0:T(8,128)(2,1)}) fusion(f32[1024,2048]{1,0:T(8,128)} %fusion.82, f32[1024,2048]{1,0:T(8,128)} %fusion.83, bf16[2048,2048]{1,0:T(8,128)(2,1)} %param.34, bf16[1024,2048]{1,0:T(8,128)(2,1)} %param.35, ...), kind=kOutput, calls=%fused_computation.30 | convolution fusion | flops 8625586176 | bytes 41944064 | tf_op jit(solution)/shard_map/dot_general | solution.py:152
  304.8 13.1 fusion.85
  317.9 13.6 convolution_add_fusion
  331.6 14.7 fusion.84
  346.3 158.2 %all-reduce.17.cloned.1.call-done = f32[1024,2048]{1,0:T(8,128)} async-done(((f32[1024,2048]{1,0:T(8,128)}), f32[1024,2048]{1,0:T(8,128)}) %all-reduce.17.cloned.1.call-update) | async-done | bytes 8388624 | tf_op jit(solution)/shard_map/psum | solution.py:162
  504.4 7.6 multiply_reduce_fusion
  512.1 9.5 multiply_add_fusion
  521.7 6.6 fusion.21
  528.8 4.0 convolution_bitcast_fusion
  532.9 7.6 multiply_convert_fusion.1
  540.5 5.6 convolution_bitcast_fusion.3
  547.8 7.4 fusion.19
  555.4 9.1 multiply_convert_fusion
  576.3 5.8 add_add_fusion
  582.9 7.2 fusion.64
  590.1 7.8 fusion.15
  598.0 7.0 fusion.66
  605.1 7.3 fusion.68
  612.6 15.6 fusion.88
  628.3 15.5 fusion.89
  644.2 15.6 fusion.62
  661.7 228.7 %all-reduce.19.cloned.1.call-done = (f32[1024,2048]{1,0:T(8,128)}, f32[1024,2048]{1,0:T(8,128)}) async-done(((f32[1024,2048]{1,0:T(8,128)}, f32[1024,2048]{1,0:T(8,128)}), (f32[1024,2048]{1,0:T(8,128)}, f32[1024,2048]{1,0:T(8,128)})) %all-reduce.19.cloned.1.call-update) | async-done | bytes 16777232 | tf_op jit(solution)/shard_map/psum | solution.py:148
  890.4 5.9 fusion.13
  896.2 29.6 %all-reduce.9 = (f32[2048]{0:T(1024)S(1)}, f32[2048]{0:T(1024)S(1)}) all-reduce(f32[2048]{0:T(1024)S(1)} %get-tuple-element.73, f32[2048]{0:T(1024)S(1)} %copy-done.47), channel_id=2, replica_groups=mesh['dp'=8,'tensor'=4] {'dp'}, use_global_device_ids=true, to_apply=%region_15.16.clone | all-reduce | flops 4096 | bytes 32768
  927.1 9.6 add_convert_fusion
  936.7 9.8 fusion.12
  946.6 49.2 %reduce-scatter.14.cloned.1.call-done = f32[512,256]{1,0:T(8,128)} async-done(((f32[512,2048]{1,0:T(8,128)}), f32[512,256]{1,0:T(8,128)}) %reduce-scatter.14.cloned.1.call-update) | async-done | bytes 524304 | tf_op jit(solution)/shard_map/reduce_scatter | solution.py:238
  995.8 51.1 %reduce-scatter.10.cloned.1.call-done = f32[256,512]{1,0:T(8,128)} async-done(((f32[2048,512]{1,0:T(8,128)}), f32[256,512]{1,0:T(8,128)}) %reduce-scatter.10.cloned.1.call-update) | async-done | bytes 524304 | tf_op jit(solution)/shard_map/reduce_scatter | solution.py:236
  1046.9 51.3 %reduce-scatter.8.cloned.1.call-done = f32[256,512]{1,0:T(8,128)} async-done(((f32[2048,512]{1,0:T(8,128)}), f32[256,512]{1,0:T(8,128)}) %reduce-scatter.8.cloned.1.call-update) | async-done | bytes 524304 | tf_op jit(solution)/shard_map/reduce_scatter | solution.py:235
  1098.2 169.6 %reduce-scatter.16.cloned.1.call-done = f32[256,2048]{1,0:T(8,128)} async-done(((f32[2048,2048]{1,0:T(8,128)}), f32[256,2048]{1,0:T(8,128)}) %reduce-scatter.16.cloned.1.call-update) | async-done | bytes 2097168 | tf_op jit(solution)/shard_map/reduce_scatter | solution.py:168
  1267.8 169.6 %reduce-scatter.18.cloned.1.call-done = f32[256,2048]{1,0:T(8,128)} async-done(((f32[2048,2048]{1,0:T(8,128)}), f32[256,2048]{1,0:T(8,128)}) %reduce-scatter.18.cloned.1.call-update) | async-done | bytes 2097168 | tf_op jit(solution)/shard_map/reduce_scatter | solution.py:169
  1437.4 169.4 %reduce-scatter.20.cloned.1.call-done = f32[2048,256]{1,0:T(8,128)} async-done(((f32[2048,2048]{1,0:T(8,128)}), f32[2048,256]{1,0:T(8,128)}) %reduce-scatter.20.cloned.1.call-update) | async-done | bytes 2097168 | tf_op jit(solution)/shard_map/reduce_scatter | solution.py:170
  (188 shorter events, 26.0 us)
Async XLA Ops:
  7.2 58.5 %copy-start = (bf16[512,2048]{1,0:T(8,128)(2,1)S(1)}, bf16[512,2048]{1,0:T(8,128)(2,1)}, u32[]{:S(2)}) copy-start(bf16[512,2048]{1,0:T(8,128)(2,1)} %param.30) | copy-start | bytes 6291460
  7.2 239.3 %all-reduce.15.cloned.1.call-start = ((), (), s32[]{:S(2)}) async-start(), calls=%async_computation.7 | async-start | bytes 16777216 | tf_op jit(solution)/shard_map/psum | solution.py:139
  17.2 17.6 %copy-start.44 = (f32[1024]{0:T(1024)}, f32[1024]{0:T(1024)S(1)}, u32[]{:S(2)}) copy-start(f32[1024]{0:T(1024)S(1)} %add_rsqrt_fusion.1) | copy-start | bytes 12292
  27.3 10.7 copy-start.9
  27.4 10.6 copy-start.11
  27.4 10.6 copy-start.13
  27.4 10.6 copy-start.15
  28.0 24.2 %copy-start.19 = (pred[512,896]{1,0:T(8,128)(4,1)}, pred[512,896]{1,0:T(8,128)(4,1)S(1)}, u32[]{:S(2)}) copy-start(pred[512,896]{1,0:T(8,128)(4,1)S(1)} %and_and_fusion.1) | copy-start | bytes 1376260
  30.8 21.4 %copy-start.5 = (f32[8,512,896]{2,1,0:T(8,128)}, f32[8,512,896]{2,1,0:T(8,128)S(1)}, u32[]{:S(2)}) copy-start(f32[8,512,896]{2,1,0:T(8,128)S(1)} %get-tuple-element.127) | copy-start | bytes 44040196
  34.8 17.4 %copy-start.52 = (f32[8,512]{1,0:T(8,128)}, f32[8,512]{1,0:T(8,128)S(1)}, u32[]{:S(2)}) copy-start(f32[8,512]{1,0:T(8,128)S(1)} %log_add_fusion.1) | copy-start | bytes 49156
  37.5 14.8 copy-start.39
  38.0 18.4 %copy-start.27 = (pred[512,896]{1,0:T(8,128)(4,1)}, pred[512,896]{1,0:T(8,128)(4,1)S(1)}, u32[]{:S(2)}) copy-start(pred[512,896]{1,0:T(8,128)(4,1)S(1)} %and_and_fusion) | copy-start | bytes 1376260
  56.4 7.5 copy-start.23
  71.5 432.9 %all-reduce.17.cloned.1.call-start = ((), (), s32[]{:S(2)}) async-start(), calls=%async_computation.8 | async-start | bytes 16777216 | tf_op jit(solution)/shard_map/psum | solution.py:162
  71.6 180.6 %copy-start.43 = (f32[2048]{0:T(1024)S(1)}, f32[2048]{0:T(1024)}, u32[]{:S(2)}) copy-start(f32[2048]{0:T(1024)} %param.31) | copy-start | bytes 24580
  252.2 17.4 %copy-start.2 = (f32[1024,2048]{1,0:T(8,128)}, f32[1024,2048]{1,0:T(8,128)S(1)}, u32[]{:S(2)}) copy-start(f32[1024,2048]{1,0:T(8,128)S(1)} %get-tuple-element.82) | copy-start | bytes 25165828
  253.0 16.6 %copy-start.17 = (bf16[1024,2048]{1,0:T(8,128)(2,1)}, bf16[1024,2048]{1,0:T(8,128)(2,1)S(1)}, u32[]{:S(2)}) copy-start(bf16[1024,2048]{1,0:T(8,128)(2,1)S(1)} %multiply_convert_fusion.5) | copy-start | bytes 12582916
  304.8 13.2 copy-start.58
  331.5 558.8 %all-reduce.19.cloned.1.call-start = ((), (), s32[]{:S(2)}) async-start(), calls=%async_computation.16 | async-start | bytes 33554432 | tf_op jit(solution)/shard_map/psum | solution.py:148
  504.4 7.6 copy-start.18
  512.1 16.7 %slice-start = ((s8[14680064]{0:T(1024)(128)(4,1)}), s8[4194304]{0:T(1024)(128)(4,1)S(1)}, s32[]{:S(2)}) async-start(s8[14680064]{0:T(1024)(128)(4,1)} %bitcast.98), calls=%async_computation.17 | async-start | bytes 8388608
  512.1 16.7 %slice-start.1 = ((s8[14680064]{0:T(1024)(128)(4,1)}), s8[4194304]{0:T(1024)(128)(4,1)S(1)}, s32[]{:S(2)}) async-start(s8[14680064]{0:T(1024)(128)(4,1)} %bitcast.98), calls=%async_computation.18 | async-start | bytes 8388608
  512.1 16.7 %slice-start.2 = ((s8[14680064]{0:T(1024)(128)(4,1)}), s8[4194304]{0:T(1024)(128)(4,1)S(1)}, s32[]{:S(2)}) async-start(s8[14680064]{0:T(1024)(128)(4,1)} %bitcast.98), calls=%async_computation.19 | async-start | bytes 8388608
  521.6 6.7 copy-start.24
  521.6 6.7 copy-start.26
  521.6 7.1 slice-start.3
  521.6 7.1 copy-start.20
  521.6 7.1 copy-start.53
  528.4 19.3 %copy-start.42 = (bf16[512,512]{0,1:T(8,128)(2,1)}, bf16[512,512]{0,1:T(8,128)(2,1)S(1)}, u32[]{:S(2)}) copy-start(bf16[512,512]{0,1:T(8,128)(2,1)S(1)} %get-tuple-element.98) | copy-start | bytes 1572868
  532.9 7.6 copy-start.8
  540.5 5.6 copy-start.10
  540.5 5.6 copy-start.12
  547.7 7.6 copy-start.38
  555.4 9.2 copy-start.14
  555.4 9.2 copy-start.16
  582.2 7.9 copy-start.32
  582.2 364.4 %reduce-scatter.12.cloned.1.call-start = ((), (), s32[]{:S(2)}) async-start(), calls=%async_computation.11 | async-start | bytes 4718592 | tf_op jit(solution)/shard_map/reduce_scatter | solution.py:237
  590.1 7.9 copy-start.36
  590.1 405.7 %reduce-scatter.14.cloned.1.call-start = ((), (), s32[]{:S(2)}) async-start(), calls=%async_computation.12 | async-start | bytes 4718592 | tf_op jit(solution)/shard_map/reduce_scatter | solution.py:238
  597.9 7.2 copy-start.34
  597.9 449.0 %reduce-scatter.10.cloned.1.call-start = ((), (), s32[]{:S(2)}) async-start(), calls=%async_computation.10 | async-start | bytes 4718592 | tf_op jit(solution)/shard_map/reduce_scatter | solution.py:236
  605.0 493.2 %reduce-scatter.8.cloned.1.call-start = ((), (), s32[]{:S(2)}) async-start(), calls=%async_computation.9 | async-start | bytes 4718592 | tf_op jit(solution)/shard_map/reduce_scatter | solution.py:235
  612.4 655.4 %reduce-scatter.16.cloned.1.call-start = ((), (), s32[]{:S(2)}) async-start(), calls=%async_computation.13 | async-start | bytes 18874368 | tf_op jit(solution)/shard_map/reduce_scatter | solution.py:168
  628.3 809.1 %reduce-scatter.18.cloned.1.call-start = ((), (), s32[]{:S(2)}) async-start(), calls=%async_computation.14 | async-start | bytes 18874368 | tf_op jit(solution)/shard_map/reduce_scatter | solution.py:169
  643.9 963.0 %reduce-scatter.20.cloned.1.call-start = ((), (), s32[]{:S(2)}) async-start(), calls=%async_computation.15 | async-start | bytes 18874368 | tf_op jit(solution)/shard_map/reduce_scatter | solution.py:170
  659.8 236.4 %copy-start.47 = (f32[2048]{0:T(1024)S(1)}, f32[2048]{0:T(1024)}, u32[]{:S(2)}) copy-start(f32[2048]{0:T(1024)} %get-tuple-element.71) | copy-start | bytes 24580
  927.1 9.6 copy-start.4
  927.1 679.7 %copy-start.1 = (bf16[512,2048]{1,0:T(8,128)(2,1)S(1)}, bf16[512,2048]{1,0:T(8,128)(2,1)}, u32[]{:S(2)}) copy-start(bf16[512,2048]{1,0:T(8,128)(2,1)} %param.30) | copy-start | bytes 6291460
  (25 other events, 68.0 us)
Sparse Core Ops, SparseCore 0:
  71.7 174.7 all-reduce.14
  331.7 172.7 all-reduce.16
  582.3 308.0 all-reduce.18
  893.1 51.4 reduce-scatter.11
  947.3 48.4 reduce-scatter.13
  998.5 48.3 reduce-scatter.9
  1049.8 48.3 reduce-scatter.7
  1101.2 166.6 reduce-scatter.15
  1270.8 166.6 reduce-scatter.17
  1440.2 166.6 reduce-scatter.19
where the time goes:
time: 1620 us; the launch traced here: 1610 us
  waiting for transfers between devices  1220 us (75%)
  matrix products  263 us (16%)
  other arithmetic  72.8 us (4%)
  blocking collectives  29.6 us (2%)
  between operations  16.4 us (1%)
    psum x1, waiting for transfers between devices, on_device(): mlp_total = lax.psum(mlp_part, 'tensor')  229 us
    psum x1, waiting for transfers between devices, on_device(): attn_total = lax.psum(attn_part, 'tensor')  175 us
    reduce_scatter x1, waiting for transfers between devices, on_device(): lax.psum_scatter(up_grad, 'dp', scatter_dimension=0, tiled=True)  170 us
    reduce_scatter x1, waiting for transfers between devices, on_device(): lax.psum_scatter(gate_grad, 'dp', scatter_dimension=0, tiled=True)  170 us
    reduce_scatter x1, waiting for transfers between devices, on_device(): lax.psum_scatter(down_grad, 'dp', scatter_dimension=1, tiled=True)  169 us
    psum x1, waiting for transfers between devices, on_device(): act_two_grad = lax.psum(act_two_part, 'tensor')  158 us
    reduce_scatter x1, waiting for transfers between devices, on_device(): lax.psum_scatter(query_grad, 'dp', scatter_dimension=0, tiled=True)  51.3 us
    reduce_scatter x1, waiting for transfers between devices, on_device(): lax.psum_scatter(key_grad, 'dp', scatter_dimension=0, tiled=True)  51.1 us
  transfers between devices with their start and end apart: 10, of which 9 were waited for; matrix products, arithmetic and copies ran while one was open for 7% of the time, Pallas kernels for 0%

commit v1 on v0

--- a/solution.py
+++ b/solution.py
@@ -159,7 +159,11 @@
     act_two_part = jnp.dot(gate_back, gate_weight.T, preferred_element_type=jnp.float32) + jnp.dot(
         up_back, up_weight.T, preferred_element_type=jnp.float32
     )
-    act_two_grad = lax.psum(act_two_part, "tensor")
+    act_two_grad = act_two_part
+    for hop in (1, 2):
+        act_two_grad = act_two_grad + lax.ppermute(
+            act_two_grad, "tensor", [(dev, dev ^ hop) for dev in range(4)]
+        )
     hidden_norm_back, second_gain_grad = rms_backward(
         hidden_sum, inverse_two, feedforward_gain, act_two_grad
     )

time: 1620 us -> 1840 us (1.14)
  waiting for transfers between devices: 1220 us -> 1410 us
    ppermute x0 -> x2, waiting for transfers between devices: none -> 344 us  [on_device(): lax.ppermute(act_two_grad, 'tensor', [(dev, dev ^ hop) for dev in range(4)])]
    psum x1 -> x0, waiting for transfers between devices: 158 us -> none  [on_device(): act_two_grad = lax.psum(act_two_part, 'tensor')]
  transfers between devices with their start and end apart: 10 -> 11, of which waited for: 9 -> 10; matrix products, arithmetic and copies ran while one was open for 7% -> 6% of each run, Pallas kernels for 0% -> 0%
where the time goes in v1:
time: 1840 us; the launch traced here: 1830 us
  waiting for transfers between devices  1410 us (77%)
  matrix products  278 us (15%)
  other arithmetic  83 us (5%)
  blocking collectives  29.6 us (2%)
    ppermute x2, waiting for transfers between devices, on_device(): lax.ppermute(act_two_grad, 'tensor', [(dev, dev ^ hop) for dev in range(4)])  344 us
    psum x1, waiting for transfers between devices, on_device(): mlp_total = lax.psum(mlp_part, 'tensor')  229 us
    psum x1, waiting for transfers between devices, on_device(): attn_total = lax.psum(attn_part, 'tensor')  175 us
    reduce_scatter x1, waiting for transfers between devices, on_device(): lax.psum_scatter(down_grad, 'dp', scatter_dimension=1, tiled=True)  170 us
    reduce_scatter x1, waiting for transfers between devices, on_device(): lax.psum_scatter(gate_grad, 'dp', scatter_dimension=0, tiled=True)  170 us
    reduce_scatter x1, waiting for transfers between devices, on_device(): lax.psum_scatter(up_grad, 'dp', scatter_dimension=0, tiled=True)  170 us
    reduce_scatter x1, waiting for transfers between devices, on_device(): lax.psum_scatter(query_grad, 'dp', scatter_dimension=0, tiled=True)  51.1 us
    reduce_scatter x1, waiting for transfers between devices, on_device(): lax.psum_scatter(key_grad, 'dp', scatter_dimension=0, tiled=True)  51.1 us
  transfers between devices with their start and end apart: 11, of which 10 were waited for; matrix products, arithmetic and copies ran while one was open for 6% of the time, Pallas kernels for 0%

profile of v1, /device:TPU:0, one launch (start us, length us, event | category | flops | bytes accessed | tf_op | source)
XLA Modules:
  0.0 1829.9 jit_solution(15961373914016344815)
XLA Ops:
  8.9 4.5 compare_select_fusion.1
  14.1 3.1 fusion.14
  17.2 5.5 fusion.72
  28.0 2.8 fusion.6
  30.8 4.1 exponential_reduce_fusion.1
  38.1 6.8 fusion.7
  44.9 7.3 exponential_reduce_fusion
  52.4 4.1 fusion.24
  56.6 18.0 fusion.25
  76.4 5.8 fusion.81
  82.3 174.8 %all-reduce.14.cloned.1.call-done = f32[1024,2048]{1,0:T(8,128)} async-done(((f32[1024,2048]{1,0:T(8,128)}), f32[1024,2048]{1,0:T(8,128)}) %all-reduce.14.cloned.1.call-update) | async-done | bytes 8388624 | tf_op jit(solution)/shard_map/psum | solution.py:139
  257.1 5.7 multiply_reduce_fusion.2
  263.7 16.6 fusion.82
  280.2 13.3 fusion.83
  293.6 21.9 %multiply_convert_fusion.2 = (bf16[1024,2048]{1,0:T(8,128)(2,1)}, bf16[1024,2048]{1,0:T(8,128)(2,1)}, bf16[1024,2048]{1,0:T(8,128)(2,1)}) fusion(f32[1024,2048]{1,0:T(8,128)} %fusion.82, f32[1024,2048]{1,0:T(8,128)} %fusion.83, bf16[2048,2048]{1,0:T(8,128)(2,1)} %param.34, bf16[1024,2048]{1,0:T(8,128)(2,1)} %param.35, ...), kind=kOutput, calls=%fused_computation.30 | convolution fusion | flops 8625586176 | bytes 41944064 | tf_op jit(solution)/shard_map/dot_general | solution.py:152
  315.5 15.3 fusion.85
  330.8 12.8 convolution_add_fusion
  347.0 178.8 %collective-permute-done = f32[1024,2048]{1,0:T(8,128)} collective-permute-done((f32[1024,2048]{1,0:T(8,128)S(1)}, f32[1024,2048]{1,0:T(8,128)}, u32[]{:S(2)}, u32[]{:S(2)}) %collective-permute-start) | collective-permute-done | bytes 8388640 | tf_op jit(solution)/shard_map/ppermute | solution.py:164
  525.8 11.9 add.249
  539.1 14.8 fusion.84
  553.9 165.4 %collective-permute-done.1 = f32[1024,2048]{1,0:T(8,128)} collective-permute-done((f32[1024,2048]{1,0:T(8,128)}, f32[1024,2048]{1,0:T(8,128)}, u32[]{:S(2)}, u32[]{:S(2)}) %collective-permute-start.1) | collective-permute-done | bytes 8388640 | tf_op jit(solution)/shard_map/ppermute | solution.py:164
  719.3 5.7 multiply_reduce_fusion
  725.0 9.6 multiply_add_fusion
  734.7 5.9 fusion.21
  741.1 7.6 convolution_bitcast_fusion
  748.7 7.5 multiply_convert_fusion.1
  756.3 5.6 convolution_bitcast_fusion.3
  763.6 7.4 fusion.19
  771.3 9.1 multiply_convert_fusion
  792.2 5.9 add_add_fusion
  798.8 7.2 fusion.64
  806.1 7.8 fusion.15
  813.9 7.0 fusion.66
  821.0 7.3 fusion.68
  828.6 15.6 fusion.88
  844.3 15.5 fusion.89
  860.1 15.6 fusion.62
  877.7 228.6 %all-reduce.16.cloned.1.call-done = (f32[1024,2048]{1,0:T(8,128)}, f32[1024,2048]{1,0:T(8,128)}) async-done(((f32[1024,2048]{1,0:T(8,128)}, f32[1024,2048]{1,0:T(8,128)}), (f32[1024,2048]{1,0:T(8,128)}, f32[1024,2048]{1,0:T(8,128)})) %all-reduce.16.cloned.1.call-update) | async-done | bytes 16777232 | tf_op jit(solution)/shard_map/psum | solution.py:148
  1106.3 5.9 fusion.13
  1112.2 29.6 %all-reduce.9 = (f32[2048]{0:T(1024)S(1)}, f32[2048]{0:T(1024)S(1)}) all-reduce(f32[2048]{0:T(1024)S(1)} %get-tuple-element.73, f32[2048]{0:T(1024)S(1)} %copy-done.49), channel_id=2, replica_groups=mesh['dp'=8,'tensor'=4] {'dp'}, use_global_device_ids=true, to_apply=%region_14.15.clone | all-reduce | flops 4096 | bytes 32768
  1143.1 9.6 add_convert_fusion
  1152.7 9.8 fusion.12
  1162.5 49.4 %reduce-scatter.14.cloned.1.call-done = f32[512,256]{1,0:T(8,128)} async-done(((f32[512,2048]{1,0:T(8,128)}), f32[512,256]{1,0:T(8,128)}) %reduce-scatter.14.cloned.1.call-update) | async-done | bytes 524304 | tf_op jit(solution)/shard_map/reduce_scatter | solution.py:242
  1211.9 51.1 %reduce-scatter.10.cloned.1.call-done = f32[256,512]{1,0:T(8,128)} async-done(((f32[2048,512]{1,0:T(8,128)}), f32[256,512]{1,0:T(8,128)}) %reduce-scatter.10.cloned.1.call-update) | async-done | bytes 524304 | tf_op jit(solution)/shard_map/reduce_scatter | solution.py:240
  1263.0 51.1 %reduce-scatter.8.cloned.1.call-done = f32[256,512]{1,0:T(8,128)} async-done(((f32[2048,512]{1,0:T(8,128)}), f32[256,512]{1,0:T(8,128)}) %reduce-scatter.8.cloned.1.call-update) | async-done | bytes 524304 | tf_op jit(solution)/shard_map/reduce_scatter | solution.py:239
  1314.2 169.6 %reduce-scatter.16.cloned.1.call-done = f32[256,2048]{1,0:T(8,128)} async-done(((f32[2048,2048]{1,0:T(8,128)}), f32[256,2048]{1,0:T(8,128)}) %reduce-scatter.16.cloned.1.call-update) | async-done | bytes 2097168 | tf_op jit(solution)/shard_map/reduce_scatter | solution.py:172
  1483.8 169.6 %reduce-scatter.18.cloned.1.call-done = f32[256,2048]{1,0:T(8,128)} async-done(((f32[2048,2048]{1,0:T(8,128)}), f32[256,2048]{1,0:T(8,128)}) %reduce-scatter.18.cloned.1.call-update) | async-done | bytes 2097168 | tf_op jit(solution)/shard_map/reduce_scatter | solution.py:173
  1653.4 169.6 %reduce-scatter.20.cloned.1.call-done = f32[2048,256]{1,0:T(8,128)} async-done(((f32[2048,2048]{1,0:T(8,128)}), f32[2048,256]{1,0:T(8,128)}) %reduce-scatter.20.cloned.1.call-update) | async-done | bytes 2097168 | tf_op jit(solution)/shard_map/reduce_scatter | solution.py:174
  (199 shorter events, 36.0 us)
Async XLA Ops:
  7.2 69.2 %copy-start = (bf16[512,2048]{1,0:T(8,128)(2,1)S(1)}, bf16[512,2048]{1,0:T(8,128)(2,1)}, u32[]{:S(2)}) copy-start(bf16[512,2048]{1,0:T(8,128)(2,1)} %param.30) | copy-start | bytes 6291460
  7.2 249.9 %all-reduce.14.cloned.1.call-start = ((), (), s32[]{:S(2)}) async-start(), calls=%async_computation.7 | async-start | bytes 16777216 | tf_op jit(solution)/shard_map/psum | solution.py:139
  17.2 17.7 copy-start.46
  27.4 10.7 copy-start.11
  27.4 10.7 copy-start.13
  27.4 10.7 copy-start.15
  27.4 10.7 copy-start.17
  28.0 24.3 %copy-start.21 = (pred[512,896]{1,0:T(8,128)(4,1)}, pred[512,896]{1,0:T(8,128)(4,1)S(1)}, u32[]{:S(2)}) copy-start(pred[512,896]{1,0:T(8,128)(4,1)S(1)} %and_and_fusion.1) | copy-start | bytes 1376260
  30.8 21.5 %copy-start.6 = (f32[8,512,896]{2,1,0:T(8,128)}, f32[8,512,896]{2,1,0:T(8,128)S(1)}, u32[]{:S(2)}) copy-start(f32[8,512,896]{2,1,0:T(8,128)S(1)} %get-tuple-element.127) | copy-start | bytes 44040196
  34.9 17.4 copy-start.54
  37.6 14.8 copy-start.41
  38.1 18.4 %copy-start.29 = (pred[512,896]{1,0:T(8,128)(4,1)}, pred[512,896]{1,0:T(8,128)(4,1)S(1)}, u32[]{:S(2)}) copy-start(pred[512,896]{1,0:T(8,128)(4,1)S(1)} %and_and_fusion) | copy-start | bytes 1376260
  56.5 18.1 copy-start.25
  82.2 1024.1 %all-reduce.16.cloned.1.call-start = ((), (), s32[]{:S(2)}) async-start(), calls=%async_computation.15 | async-start | bytes 33554432 | tf_op jit(solution)/shard_map/psum | solution.py:148
  82.2 180.6 %copy-start.45 = (f32[2048]{0:T(1024)S(1)}, f32[2048]{0:T(1024)}, u32[]{:S(2)}) copy-start(f32[2048]{0:T(1024)} %param.31) | copy-start | bytes 24580
  262.8 17.4 copy-start.2
  263.7 16.6 copy-start.20
  315.5 15.3 copy-start.60
  343.6 182.2 %collective-permute-start = (f32[1024,2048]{1,0:T(8,128)S(1)}, f32[1024,2048]{1,0:T(8,128)}, u32[]{:S(2)}, u32[]{:S(2)}) collective-permute-start(f32[1024,2048]{1,0:T(8,128)S(1)} %convolution_add_fusion), channel_id=1, source_target_pairs={{0,1},{1,0},{2,3},{3,2},{4,5},{5,4},{6,7},{7,6},{8,9},{9,8},{10,11... | collective-permute-start | bytes 25165832 | tf_op jit(solution)/shard_map/ppermute | solution.py:164
  525.8 193.4 %slice-start = ((s8[8388608]{0:T(1024)(128)(4,1)}), s8[4194304]{0:T(1024)(128)(4,1)S(1)}, s32[]{:S(2)}) async-start(s8[8388608]{0:T(1024)(128)(4,1)} %bitcast.98), calls=%async_computation.16 | async-start | bytes 8388608
  537.8 181.5 %collective-permute-start.1 = (f32[1024,2048]{1,0:T(8,128)}, f32[1024,2048]{1,0:T(8,128)}, u32[]{:S(2)}, u32[]{:S(2)}) collective-permute-start(f32[1024,2048]{1,0:T(8,128)} %add.249), channel_id=1, source_target_pairs={{0,2},{1,3},{2,0},{3,1},{4,6},{5,7},{6,4},{7,5},{8,10},{9,11},{10,... | collective-permute-start | bytes 25165832 | tf_op jit(solution)/shard_map/ppermute | solution.py:164
  539.1 180.2 %slice-start.1 = ((s8[8388608]{0:T(1024)(128)(4,1)}), s8[4194304]{0:T(1024)(128)(4,1)S(1)}, s32[]{:S(2)}) async-start(s8[8388608]{0:T(1024)(128)(4,1)} %bitcast.98), calls=%async_computation.17 | async-start | bytes 8388608
  539.1 180.2 %copy-start.3 = (f32[1024,2048]{1,0:T(8,128)S(1)}, f32[1024,2048]{1,0:T(8,128)}, u32[]{:S(2)}) copy-start(f32[1024,2048]{1,0:T(8,128)} %add.249) | copy-start | bytes 25165828
  553.9 171.1 %copy-start.19 = (bf16[1024,2048]{1,0:T(8,128)(2,1)S(1)}, bf16[1024,2048]{1,0:T(8,128)(2,1)}, u32[]{:S(2)}) copy-start(bf16[1024,2048]{1,0:T(8,128)(2,1)} %param.35) | copy-start | bytes 12582916
  734.6 6.4 copy-start.55
  734.7 14.0 slice-start.2
  734.7 14.0 slice-start.3
  740.7 22.9 %copy-start.44 = (bf16[512,512]{0,1:T(8,128)(2,1)}, bf16[512,512]{0,1:T(8,128)(2,1)S(1)}, u32[]{:S(2)}) copy-start(bf16[512,512]{0,1:T(8,128)(2,1)S(1)} %get-tuple-element.98) | copy-start | bytes 1572868
  740.7 8.0 slice-start.4
  741.1 7.6 slice-start.5
  741.1 7.6 copy-start.42
  748.7 7.5 copy-start.9
  763.6 7.6 copy-start.40
  771.2 9.2 copy-start.16
  771.2 9.2 copy-start.18
  798.1 8.0 copy-start.34
  798.1 364.4 %reduce-scatter.12.cloned.1.call-start = ((), (), s32[]{:S(2)}) async-start(), calls=%async_computation.10 | async-start | bytes 4718592 | tf_op jit(solution)/shard_map/reduce_scatter | solution.py:241
  806.0 7.9 copy-start.38
  806.0 405.9 %reduce-scatter.14.cloned.1.call-start = ((), (), s32[]{:S(2)}) async-start(), calls=%async_computation.11 | async-start | bytes 4718592 | tf_op jit(solution)/shard_map/reduce_scatter | solution.py:242
  813.9 7.1 copy-start.36
  813.9 449.2 %reduce-scatter.10.cloned.1.call-start = ((), (), s32[]{:S(2)}) async-start(), calls=%async_computation.9 | async-start | bytes 4718592 | tf_op jit(solution)/shard_map/reduce_scatter | solution.py:240
  821.0 493.2 %reduce-scatter.8.cloned.1.call-start = ((), (), s32[]{:S(2)}) async-start(), calls=%async_computation.8 | async-start | bytes 4718592 | tf_op jit(solution)/shard_map/reduce_scatter | solution.py:239
  828.3 655.4 %reduce-scatter.16.cloned.1.call-start = ((), (), s32[]{:S(2)}) async-start(), calls=%async_computation.12 | async-start | bytes 18874368 | tf_op jit(solution)/shard_map/reduce_scatter | solution.py:172
  844.3 809.1 %reduce-scatter.18.cloned.1.call-start = ((), (), s32[]{:S(2)}) async-start(), calls=%async_computation.13 | async-start | bytes 18874368 | tf_op jit(solution)/shard_map/reduce_scatter | solution.py:173
  859.8 963.1 %reduce-scatter.20.cloned.1.call-start = ((), (), s32[]{:S(2)}) async-start(), calls=%async_computation.14 | async-start | bytes 18874368 | tf_op jit(solution)/shard_map/reduce_scatter | solution.py:174
  875.8 236.4 %copy-start.49 = (f32[2048]{0:T(1024)S(1)}, f32[2048]{0:T(1024)}, u32[]{:S(2)}) copy-start(f32[2048]{0:T(1024)} %get-tuple-element.71) | copy-start | bytes 24580
  1143.1 9.6 copy-start.5
  1143.1 679.9 %copy-start.1 = (bf16[512,2048]{1,0:T(8,128)(2,1)S(1)}, bf16[512,2048]{1,0:T(8,128)(2,1)}, u32[]{:S(2)}) copy-start(bf16[512,2048]{1,0:T(8,128)(2,1)} %param.30) | copy-start | bytes 6291460
  (30 other events, 97.2 us)
Sparse Core Ops, SparseCore 0:
  82.3 174.7 all-reduce.13
  798.2 308.0 all-reduce.15
  1109.2 51.4 reduce-scatter.11
  1163.4 48.4 reduce-scatter.13
  1214.6 48.3 reduce-scatter.9
  1265.8 48.3 reduce-scatter.7
  1317.1 166.6 reduce-scatter.15
  1486.7 166.6 reduce-scatter.17
  1656.3 166.6 reduce-scatter.19
